TPU v7x, 32 devices: a whole 2x2x4 slice. The times are simulated.
32 devices in a mesh: dp: 2 (over x), hst: 4 (over y, core), chip: 4 (over z).
Axes of the slice: x: 2, y: 2, z: 4, core: 2. Of those that a mesh axis runs over, the one named last changes fastest.
Arguments:
- tokens: bfloat16 [512, 8192], P('dp', ('hst', 'chip')), may hold values from -6 to 6
- out_grad: bfloat16 [512, 8192], P('dp', ('hst', 'chip')), may hold values from -6 to 6
- up_blocks: bfloat16 [112, 16, 128, 128], P(('hst', 'chip')), may hold values from -0.125 to 0.125
- up_cols: int32 [112, 16], P(('hst', 'chip')), may hold values from 0 to 63, all different within a row
- down_blocks: bfloat16 [112, 16, 128, 128], P(('hst', 'chip')), may hold values from -0.09375 to 0.09375
- down_cols: int32 [112, 16], P(('hst', 'chip')), may hold values from 0 to 63, all different within a row
Outputs:
- input_grad: bfloat16 [512, 8192], P('dp', ('hst', 'chip'))
- up_grad: float32 [112, 16, 128, 128], P(('hst', 'chip'), None, 'dp')
- down_grad: float32 [112, 16, 128, 128], P(('hst', 'chip'), None, 'dp')
Inputs may be any that keep to these rules, and one draw needn't show every extreme that they name: `up_cols`: each block row names 16 different block columns; every block column is named by some row. `down_cols`: each block row names 16 different block columns; every block column is named by some row.
All inputs are finite; a program needn't handle non-finite values.
Results may differ from a plain program's by a relative error of at most 0.017.
Values may be sent and summed in bfloat16 or wider, within the bound.
A program may use at most 128 MiB of HBM per device.

v0:
```python
import jax
import jax.numpy as jnp
from jax import lax
from jax.sharding import PartitionSpec as P


def local(tokens, out_grad, up_blocks, up_cols, down_blocks, down_cols):
    whole_x, whole_dy = (
        lax.all_gather(tokens, ("hst", "chip"), axis=1, tiled=True),
        lax.all_gather(out_grad, ("hst", "chip"), axis=1, tiled=True),
    )
    tok_rows = whole_x.shape[0]
    block_size = up_blocks.shape[2]
    local_rows = up_blocks.shape[0]
    dblocks = whole_x.shape[1] // block_size
    x_blocks = whole_x.reshape(tok_rows, dblocks, block_size)
    dy_blocks = whole_dy.reshape(tok_rows, dblocks, block_size)
    x_sel = x_blocks[:, up_cols, :]
    dy_sel = dy_blocks[:, down_cols, :]
    pre_act = jnp.einsum("tjkc,jkhc->tjh", x_sel, up_blocks, preferred_element_type=jnp.float32)
    activated = jax.nn.silu(pre_act).astype(jnp.bfloat16)
    down_part = jnp.einsum("tjh,tjkc->jkhc", activated, dy_sel, preferred_element_type=jnp.float32)
    hidden_grad = jnp.einsum(
        "tjkc,jkhc->tjh", dy_sel, down_blocks, preferred_element_type=jnp.float32
    )
    sigmoid_pre = jax.nn.sigmoid(pre_act)
    pre_grad = (hidden_grad * sigmoid_pre * (1.0 + pre_act * (1.0 - sigmoid_pre))).astype(
        jnp.bfloat16
    )
    up_part = jnp.einsum("tjh,tjkc->jkhc", pre_grad, x_sel, preferred_element_type=jnp.float32)
    up_sum, down_sum = (
        lax.psum_scatter(
            up_part.astype(jnp.bfloat16), "dp", scatter_dimension=2, tiled=True
        ).astype(jnp.float32),
        lax.psum_scatter(
            down_part.astype(jnp.bfloat16), "dp", scatter_dimension=2, tiled=True
        ).astype(jnp.float32),
    )
    onehot = (up_cols[:, :, None] == jnp.arange(dblocks, dtype=jnp.int32)[None, None, :]).astype(
        jnp.bfloat16
    )
    dense_up = jnp.einsum(
        "jkb,jkhc->jhbc", onehot, up_blocks, preferred_element_type=jnp.float32
    ).astype(jnp.bfloat16)
    dense_up = dense_up.reshape(local_rows * block_size, dblocks * block_size)
    flat_grad = pre_grad.reshape(tok_rows, local_rows * block_size)
    partial_value = jnp.dot(flat_grad, dense_up, preferred_element_type=jnp.float32)
    summed = lax.psum_scatter(
        partial_value.astype(jnp.bfloat16), ("hst", "chip"), scatter_dimension=1, tiled=True
    )
    return (summed, up_sum, down_sum)


def solution(mesh):
    placed = (
        P("dp", ("hst", "chip")),
        P("dp", ("hst", "chip")),
        P(("hst", "chip"), None, None, None),
        P(("hst", "chip"), None),
        P(("hst", "chip"), None, None, None),
        P(("hst", "chip"), None),
    )
    return jax.shard_map(
        local,
        mesh=mesh,
        in_specs=placed,
        out_specs=(
            P("dp", ("hst", "chip")),
            P(("hst", "chip"), None, "dp", None),
            P(("hst", "chip"), None, "dp", None),
        ),
        check_vma=False,
    )
```

profile of v0, /device:TPU:0, one launch (start us, length us, event | category | flops | bytes accessed | tf_op | source)
XLA Modules:
  0.0 353.4 jit_solution(15198662633239594076)
XLA Ops:
  7.2 0.0 all-gather.5.cloned.1.call-start
  7.2 1.8 copy.44
  9.0 0.0 all-gather.3.cloned.1.call-start
  9.1 1.8 copy.40
  10.9 0.0 reduce-scatter.6.cloned.1.call-start
  10.9 0.7 compare_select_fusion.1
  11.6 0.1 reshape.25
  11.7 0.7 compare_select_fusion
  12.4 0.1 reshape.33
  12.5 51.4 %all-gather.5.cloned.1.call-done = bf16[256,8192]{0,1:T(8,128)(2,1)} async-done(((bf16[256,512]{0,1:T(8,128)(2,1)}), bf16[256,8192]{0,1:T(8,128)(2,1)}) %all-gather.5.cloned.1.call-update) | async-done | bytes 4194320 | tf_op jit(solution)/shard_map/all_gather | solution.py:9
  63.9 6.4 %copy.45 = bf16[256,64,128]{2,0,1:T(8,128)(2,1)} copy(bf16[256,64,128]{0,2,1:T(8,128)(2,1)} %bitcast.74) | data formatting | bytes 8388608 | tf_op jit(solution)/shard_map/reshape | solution.py:16
  70.2 45.3 %all-gather.3.cloned.1.call-done = bf16[256,8192]{0,1:T(8,128)(2,1)} async-done(((bf16[256,512]{0,1:T(8,128)(2,1)}), bf16[256,8192]{0,1:T(8,128)(2,1)}) %all-gather.3.cloned.1.call-update) | async-done | bytes 4194320 | tf_op jit(solution)/shard_map/all_gather | solution.py:10
  115.6 6.4 %copy.41 = bf16[256,64,128]{2,0,1:T(8,128)(2,1)} copy(bf16[256,64,128]{0,2,1:T(8,128)(2,1)} %bitcast.75) | data formatting | bytes 8388608 | tf_op jit(solution)/shard_map/reshape | solution.py:17
  122.0 8.5 %gather_fusion.1 = bf16[112,256,128]{2,1,0:T(8,128)(2,1)} fusion(bf16[256,64,128]{2,0,1:T(8,128)(2,1)} %copy.45, s32[1024]{0:T(1024)S(1)} %pad_clamp_fusion), kind=kCustom, calls=%fused_computation.1 | custom fusion | bytes 14680512 | tf_op jit(solution)/shard_map/gather | solution.py:18
  130.5 11.3 %copy.46 = bf16[7,16,256,128]{2,3,1,0:T(8,128)(2,1)} copy(bf16[7,16,256,128]{3,2,1,0:T(8,128)(2,1)} %bitcast.67) | data formatting | bytes 14680064 | tf_op jit(solution)/shard_map/gather | solution.py:18
  141.8 8.5 %gather_fusion = bf16[112,256,128]{2,1,0:T(8,128)(2,1)} fusion(bf16[256,64,128]{2,0,1:T(8,128)(2,1)} %copy.41, s32[1024]{0:T(1024)S(1)} %pad_clamp_fusion.1), kind=kCustom, calls=%fused_computation | custom fusion | bytes 14680512 | tf_op jit(solution)/shard_map/gather | solution.py:19
  150.3 6.8 %convolution_bitcast_fusion = f32[256,7,128]{0,2,1:T(8,128)S(1)} fusion(bf16[7,16,128,128]{3,2,1,0:T(8,128)(2,1)} %param.8, bf16[256,7,16,128]{3,0,2,1:T(8,128)(2,1)} %bitcast.68), kind=kOutput, calls=%fused_computation.14 | convolution fusion | flops 939524096 | bytes 11927552 | tf_op jit(solution)/shard_map/tjkc,jkhc->tjh/dot_general | solution.py:20
  157.1 0.5 copy-done.2
  157.6 2.5 fusion.17
  160.1 3.9 %convert_bitcast_fusion.1 = bf16[7,16,128,128]{2,3,1,0:T(8,128)(2,1)} fusion(bf16[7,16,256,128]{2,3,1,0:T(8,128)(2,1)S(1)} %bitcast.70, bf16[256,7,128]{0,2,1:T(8,128)(2,1)S(1)} %fusion.17), kind=kOutput, calls=%fused_computation.13 | convolution fusion | flops 941359104 | bytes 11468800 | tf_op jit(solution)/shard_map/tjh,tjkc->jkhc/dot_general | solution.py:30
  164.1 6.5 %copy.50 = bf16[7,16,128,128]{3,1,0,2:T(8,128)(2,1)} copy(bf16[7,16,128,128]{2,3,1,0:T(8,128)(2,1)} %convert_bitcast_fusion.1) | data formatting | bytes 7340032 | tf_op jit(solution)/shard_map/convert_element_type | solution.py:33
  170.6 0.2 reduce-scatter.8.cloned.1.call-start
  170.8 11.6 %copy.42 = bf16[7,16,256,128]{2,3,1,0:T(8,128)(2,1)} copy(bf16[7,16,256,128]{3,2,1,0:T(8,128)(2,1)} %bitcast.71) | data formatting | bytes 14680064 | tf_op jit(solution)/shard_map/gather | solution.py:19
  182.4 7.0 %convert_bitcast_fusion = bf16[7,16,128,128]{2,3,1,0:T(8,128)(2,1)} fusion(bf16[7,16,256,128]{2,3,1,0:T(8,128)(2,1)} %copy.42, f32[256,7,128]{0,2,1:T(8,128)S(1)} %convolution_bitcast_fusion), kind=kOutput, calls=%fused_computation.12 | convolution fusion | flops 942505984 | bytes 11927552 | tf_op jit(solution)/shard_map/tjh,tjkc->jkhc/dot_general | solution.py:22
  189.4 6.6 %copy.52 = bf16[7,16,128,128]{3,1,0,2:T(8,128)(2,1)} copy(bf16[7,16,128,128]{2,3,1,0:T(8,128)(2,1)} %convert_bitcast_fusion) | data formatting | bytes 7340032 | tf_op jit(solution)/shard_map/convert_element_type | solution.py:36
  196.0 0.0 reduce-scatter.4.cloned.1.call-start
  196.1 11.3 %convolution_convert_fusion = bf16[7,64,128,128]{3,1,2,0:T(8,128)(2,1)} fusion(bf16[7,16,128,128]{3,2,1,0:T(8,128)(2,1)} %param.8, s32[7,16]{1,0:T(8,128)S(1)} %copy-done.1), kind=kOutput, calls=%fused_computation.6 | convolution fusion | flops 242228224 | bytes 18350528 | tf_op jit(solution)/shard_map/jkb,jkhc->jhbc/dot_general | solution.py:42
  207.4 17.7 %fusion.3 = bf16[256,8192]{1,0:T(8,128)(2,1)} fusion(bf16[256,896]{0,1:T(8,128)(2,1)S(1)} %bitcast.76, bf16[112,8,64,128]{3,2,1,0:T(8,128)(2,1)} %bitcast.73), kind=kOutput, calls=%fused_computation.5 | convolution fusion | flops 3760193536 | bytes 19333120 | tf_op jit(solution)/shard_map/dot_general | solution.py:47
  225.2 4.1 %copy.53 = f32[7,16,64,128]{3,2,1,0:T(8,128)} copy(bf16[7,16,64,128]{3,1,0,2:T(8,128)(2,1)} %reduce-scatter.6.cloned.1.call-done) | data formatting | bytes 5505024
  229.3 40.4 %reduce-scatter.8.cloned.1.call-done = bf16[7,16,64,128]{3,1,0,2:T(8,128)(2,1)} async-done(((bf16[7,16,128,128]{3,1,0,2:T(8,128)(2,1)}), bf16[7,16,64,128]{3,1,0,2:T(8,128)(2,1)}) %reduce-scatter.8.cloned.1.call-update) | async-done | bytes 1835024 | tf_op jit(solution)/shard_map/reduce_scatter | solution.py:35
  269.7 3.9 %copy.54 = f32[7,16,64,128]{3,2,1,0:T(8,128)} copy(bf16[7,16,64,128]{3,1,0,2:T(8,128)(2,1)} %reduce-scatter.8.cloned.1.call-done) | data formatting | bytes 5505024
  273.6 73.3 %reduce-scatter.4.cloned.1.call-done = bf16[256,512]{1,0:T(8,128)(2,1)} async-done(((bf16[256,8192]{1,0:T(8,128)(2,1)}), bf16[256,512]{1,0:T(8,128)(2,1)}) %reduce-scatter.4.cloned.1.call-update) | async-done | bytes 262160 | tf_op jit(solution)/shard_map/reduce_scatter | solution.py:48
  (18 shorter events, 0.1 us)
Async XLA Ops:
  7.2 56.7 %all-gather.5.cloned.1.call-start = ((), (), s32[]{:S(2)}) async-start(), calls=%async_computation.4 | async-start | bytes 4456448 | tf_op jit(solution)/shard_map/all_gather | solution.py:9
  9.0 106.6 %all-gather.3.cloned.1.call-start = ((), (), s32[]{:S(2)}) async-start(), calls=%async_computation.3 | async-start | bytes 4456448 | tf_op jit(solution)/shard_map/all_gather | solution.py:10
  10.9 214.3 %reduce-scatter.6.cloned.1.call-start = ((), (), s32[]{:S(2)}) async-start(), calls=%async_computation.6 | async-start | bytes 5505024 | tf_op jit(solution)/shard_map/reduce_scatter | solution.py:32
  150.3 6.8 %copy-start = (bf16[112,256,128]{2,1,0:T(8,128)(2,1)S(1)}, bf16[112,256,128]{2,1,0:T(8,128)(2,1)}, u32[]{:S(2)}) copy-start(bf16[112,256,128]{2,1,0:T(8,128)(2,1)} %gather_fusion) | copy-start | bytes 22020100
  150.3 7.3 %copy-start.2 = (bf16[7,16,128,128]{3,2,1,0:T(8,128)(2,1)S(1)}, bf16[7,16,128,128]{3,2,1,0:T(8,128)(2,1)}, u32[]{:S(2)}) copy-start(bf16[7,16,128,128]{3,2,1,0:T(8,128)(2,1)} %param.10) | copy-start | bytes 11010052
  150.3 9.8 %slice-start = ((s8[7340032]{0:T(1024)(128)(4,1)}), s8[4194304]{0:T(1024)(128)(4,1)S(1)}, s32[]{:S(2)}) async-start(s8[7340032]{0:T(1024)(128)(4,1)} %bitcast.69), calls=%async_computation.8 | async-start | bytes 8388608
  157.6 2.5 slice-start.1
  170.6 99.2 %reduce-scatter.8.cloned.1.call-start = ((), (), s32[]{:S(2)}) async-start(), calls=%async_computation.7 | async-start | bytes 5505024 | tf_op jit(solution)/shard_map/reduce_scatter | solution.py:35
  189.4 6.7 %copy-start.1 = (s32[7,16]{1,0:T(8,128)S(1)}, s32[7,16]{1,0:T(8,128)}, u32[]{:S(2)}) copy-start(s32[7,16]{1,0:T(8,128)} %param.9) | copy-start | bytes 1348
  196.0 150.8 %reduce-scatter.4.cloned.1.call-start = ((), (), s32[]{:S(2)}) async-start(), calls=%async_computation.5 | async-start | bytes 4456448 | tf_op jit(solution)/shard_map/reduce_scatter | solution.py:48
Sparse Core Ops, SparseCore 0:
  10.8 53.0 all-gather.4
  66.7 48.8 all-gather.2
  170.7 47.7 reduce-scatter.5
  220.5 49.1 reduce-scatter.7
  274.0 72.8 reduce-scatter.3
where the time goes:
time: 355 us; the launch traced here: 353 us
  waiting for transfers between devices  210 us (59%)
  local copies, waits for them, and re-layouts  78 us (22%)
  matrix products  49.3 us (14%)
  between operations  13.9 us (4%)
    reduce_scatter x1, waiting for transfers between devices, local(): lax.psum_scatter(partial_value.astype(jnp.bfloat16), ('hst', 'chip'), sca...  73.3 us
    all_gather x1, waiting for transfers between devices, local(): lax.all_gather(tokens, ('hst', 'chip'), axis=1, tiled=True)  51.4 us
    all_gather x1, waiting for transfers between devices, local(): lax.all_gather(out_grad, ('hst', 'chip'), axis=1, tiled=True)  45.3 us
    reduce_scatter x1, waiting for transfers between devices, local(): lax.psum_scatter(down_part.astype(jnp.bfloat16), 'dp', scatter_dimension=...  40.4 us
    gather x2, local copies, waits for them, and re-layouts, local(): dy_sel = dy_blocks[:, down_cols, :]  20 us
    gather x2, local copies, waits for them, and re-layouts, local(): x_sel = x_blocks[:, up_cols, :]  19.8 us
    dot_general x1, matrix products, local(): jnp.dot(flat_grad, dense_up, preferred_element_type=jnp.float32)  17.7 us
    unnamed x14, local copies, waits for them, and re-layouts  12.1 us
  transfers between devices with their start and end apart: 5, of which 4 were waited for; matrix products, arithmetic and copies ran while one was open for 20% of the time, Pallas kernels for 0%

commit v1 on v0

--- a/solution.py
+++ b/solution.py
@@ -4,10 +4,22 @@
 from jax.sharding import PartitionSpec as P
 
 
+def ring_gather(value, axis, dim):
+    ways, here, step = (lax.axis_size(axis), lax.axis_index(axis), value.shape[dim])
+    shape = [n * ways if d == dim else n for d, n in enumerate(value.shape)]
+    full = lax.dynamic_update_slice_in_dim(
+        jnp.zeros(shape, value.dtype), value, here * step, axis=dim
+    )
+    for far in range(1, ways):
+        value = lax.ppermute(value, axis, [(d, (d + 1) % ways) for d in range(ways)])
+        full = lax.dynamic_update_slice_in_dim(full, value, (here - far) % ways * step, axis=dim)
+    return full
+
+
 def local(tokens, out_grad, up_blocks, up_cols, down_blocks, down_cols):
     whole_x, whole_dy = (
         lax.all_gather(tokens, ("hst", "chip"), axis=1, tiled=True),
-        lax.all_gather(out_grad, ("hst", "chip"), axis=1, tiled=True),
+        ring_gather(out_grad, ("hst", "chip"), 1),
     )
     tok_rows = whole_x.shape[0]
     block_size = up_blocks.shape[2]

time: 355 us -> 415 us (1.17)
  waiting for transfers between devices: 210 us -> 253 us
  local copies, waits for them, and re-layouts: 78 us -> 91.1 us
    ppermute x0 -> x15, waiting for transfers between devices: none -> 143 us  [ring_gather(): lax.ppermute(value, axis, [(d, (d + 1) % ways) for d in range(ways)])]
    all_gather x1, waiting for transfers between devices: 51.4 us -> 0.01 us  [local(): lax.all_gather(tokens, ('hst', 'chip'), axis=1, tiled=True)]
    all_gather x1 -> x0, waiting for transfers between devices: 45.3 us -> none  [local(): lax.all_gather(out_grad, ('hst', 'chip'), axis=1, tiled=True)]
    reduce_scatter x1, waiting for transfers between devices: 40.4 us -> 0.02 us  [local(): lax.psum_scatter(down_part.astype(jnp.bfloat16), 'dp', scatter_dimension=...]
    reduce_scatter x1, waiting for transfers between devices: 0.02 us -> 36.9 us  [local(): lax.psum_scatter(up_part.astype(jnp.bfloat16), 'dp', scatter_dimension=2,...]
    dynamic_update_slice x0 -> x16, local copies, waits for them, and re-layouts: none -> 11.5 us  [the longest x15 10.8 us: ring_gather(): lax.dynamic_update_slice_in_dim(full, value, (here - far) % ways * step,...]
    dot_general x1, matrix products: 2.51 us -> 6.84 us  [local(): jnp.einsum('tjkc,jkhc->tjh', dy_sel, down_blocks, preferred_element_type=...]
    unnamed x14 -> x16, local copies, waits for them, and re-layouts: 12.1 us -> 11.5 us
  transfers between devices with their start and end apart: 5 -> 19, of which waited for: 4 -> 17; matrix products, arithmetic and copies ran while one was open for 20% -> 26% of each run, Pallas kernels for 0% -> 0%
where the time goes in v1:
time: 415 us; the launch traced here: 413 us
  waiting for transfers between devices  253 us (61%)
  local copies, waits for them, and re-layouts  91.1 us (22%)
  matrix products  50.4 us (12%)
  between operations  14.2 us (3%)
    ppermute x15, waiting for transfers between devices, ring_gather(): lax.ppermute(value, axis, [(d, (d + 1) % ways) for d in range(ways)])  143 us
    reduce_scatter x1, waiting for transfers between devices, local(): lax.psum_scatter(partial_value.astype(jnp.bfloat16), ('hst', 'chip'), sca...  73.2 us
    reduce_scatter x1, waiting for transfers between devices, local(): lax.psum_scatter(up_part.astype(jnp.bfloat16), 'dp', scatter_dimension=2,...  36.9 us
    gather x2, local copies, waits for them, and re-layouts, local(): x_sel = x_blocks[:, up_cols, :]  20.1 us
    gather x2, local copies, waits for them, and re-layouts, local(): dy_sel = dy_blocks[:, down_cols, :]  19.7 us
    dot_general x1, matrix products, local(): jnp.dot(flat_grad, dense_up, preferred_element_type=jnp.float32)  17.6 us
    unnamed x16, local copies, waits for them, and re-layouts  11.5 us
    dot_general x1, matrix products, local(): jnp.einsum('jkb,jkhc->jhbc', onehot, up_blocks, preferred_element_type=jn...  11.3 us
  transfers between devices with their start and end apart: 19, of which 17 were waited for; matrix products, arithmetic and copies ran while one was open for 26% of the time, Pallas kernels for 0%

profile of v1, /device:TPU:0, one launch (start us, length us, event | category | flops | bytes accessed | tf_op | source)
XLA Modules:
  0.0 413.2 jit_solution(3387250204908954394)
XLA Ops:
  13.3 8.4 %collective-permute-done = bf16[256,512]{0,1:T(8,128)(2,1)S(1)} collective-permute-done((bf16[256,512]{0,1:T(8,128)(2,1)S(1)}, bf16[256,512]{0,1:T(8,128)(2,1)S(1)}, u32[]{:S(2)}, u32[]{:S(2)}) %collective-permute-start) | collective-permute-done | bytes 262176 | tf_op jit(solution)/shard_map/ppermute | solution.py:14
  21.7 16.8 %collective-permute-done.1 = bf16[256,512]{0,1:T(8,128)(2,1)S(1)} collective-permute-done((bf16[256,512]{0,1:T(8,128)(2,1)S(1)}, bf16[256,512]{0,1:T(8,128)(2,1)S(1)}, u32[]{:S(2)}, u32[]{:S(2)}) %collective-permute-start.1) | collective-permute-done | bytes 262176 | tf_op jit(solution)/shard_map/ppermute | solution.py:14
  38.5 10.9 %collective-permute-done.2 = bf16[256,512]{0,1:T(8,128)(2,1)S(1)} collective-permute-done((bf16[256,512]{0,1:T(8,128)(2,1)S(1)}, bf16[256,512]{0,1:T(8,128)(2,1)S(1)}, u32[]{:S(2)}, u32[]{:S(2)}) %collective-permute-start.2) | collective-permute-done | bytes 262176 | tf_op jit(solution)/shard_map/ppermute | solution.py:14
  49.4 16.5 %collective-permute-done.3 = bf16[256,512]{0,1:T(8,128)(2,1)S(1)} collective-permute-done((bf16[256,512]{0,1:T(8,128)(2,1)S(1)}, bf16[256,512]{0,1:T(8,128)(2,1)S(1)}, u32[]{:S(2)}, u32[]{:S(2)}) %collective-permute-start.3) | collective-permute-done | bytes 262176 | tf_op jit(solution)/shard_map/ppermute | solution.py:14
  65.9 11.7 %collective-permute-done.4 = bf16[256,512]{0,1:T(8,128)(2,1)S(1)} collective-permute-done((bf16[256,512]{0,1:T(8,128)(2,1)S(1)}, bf16[256,512]{0,1:T(8,128)(2,1)S(1)}, u32[]{:S(2)}, u32[]{:S(2)}) %collective-permute-start.4) | collective-permute-done | bytes 262176 | tf_op jit(solution)/shard_map/ppermute | solution.py:14
  77.6 10.8 %collective-permute-done.5 = bf16[256,512]{0,1:T(8,128)(2,1)S(1)} collective-permute-done((bf16[256,512]{0,1:T(8,128)(2,1)S(1)}, bf16[256,512]{0,1:T(8,128)(2,1)S(1)}, u32[]{:S(2)}, u32[]{:S(2)}) %collective-permute-start.5) | collective-permute-done | bytes 262176 | tf_op jit(solution)/shard_map/ppermute | solution.py:14
  88.4 10.2 %collective-permute-done.6 = bf16[256,512]{0,1:T(8,128)(2,1)S(1)} collective-permute-done((bf16[256,512]{0,1:T(8,128)(2,1)S(1)}, bf16[256,512]{0,1:T(8,128)(2,1)S(1)}, u32[]{:S(2)}, u32[]{:S(2)}) %collective-permute-start.6) | collective-permute-done | bytes 262176 | tf_op jit(solution)/shard_map/ppermute | solution.py:14
  98.6 9.6 %collective-permute-done.7 = bf16[256,512]{0,1:T(8,128)(2,1)S(1)} collective-permute-done((bf16[256,512]{0,1:T(8,128)(2,1)S(1)}, bf16[256,512]{0,1:T(8,128)(2,1)S(1)}, u32[]{:S(2)}, u32[]{:S(2)}) %collective-permute-start.7) | collective-permute-done | bytes 262176 | tf_op jit(solution)/shard_map/ppermute | solution.py:14
  108.2 9.0 %collective-permute-done.8 = bf16[256,512]{0,1:T(8,128)(2,1)S(1)} collective-permute-done((bf16[256,512]{0,1:T(8,128)(2,1)S(1)}, bf16[256,512]{0,1:T(8,128)(2,1)S(1)}, u32[]{:S(2)}, u32[]{:S(2)}) %collective-permute-start.8) | collective-permute-done | bytes 262176 | tf_op jit(solution)/shard_map/ppermute | solution.py:14
  121.0 4.7 %collective-permute-done.9 = bf16[256,512]{0,1:T(8,128)(2,1)S(1)} collective-permute-done((bf16[256,512]{0,1:T(8,128)(2,1)S(1)}, bf16[256,512]{0,1:T(8,128)(2,1)S(1)}, u32[]{:S(2)}, u32[]{:S(2)}) %collective-permute-start.9) | collective-permute-done | bytes 262176 | tf_op jit(solution)/shard_map/ppermute | solution.py:14
  127.5 6.7 %collective-permute-done.10 = bf16[256,512]{0,1:T(8,128)(2,1)S(1)} collective-permute-done((bf16[256,512]{0,1:T(8,128)(2,1)S(1)}, bf16[256,512]{0,1:T(8,128)(2,1)S(1)}, u32[]{:S(2)}, u32[]{:S(2)}) %collective-permute-start.10) | collective-permute-done | bytes 262176 | tf_op jit(solution)/shard_map/ppermute | solution.py:14
  136.4 6.3 %collective-permute-done.11 = bf16[256,512]{0,1:T(8,128)(2,1)S(1)} collective-permute-done((bf16[256,512]{0,1:T(8,128)(2,1)S(1)}, bf16[256,512]{0,1:T(8,128)(2,1)S(1)}, u32[]{:S(2)}, u32[]{:S(2)}) %collective-permute-start.11) | collective-permute-done | bytes 262176 | tf_op jit(solution)/shard_map/ppermute | solution.py:14
  144.9 7.2 %collective-permute-done.12 = bf16[256,512]{0,1:T(8,128)(2,1)S(1)} collective-permute-done((bf16[256,512]{0,1:T(8,128)(2,1)S(1)}, bf16[256,512]{0,1:T(8,128)(2,1)S(1)}, u32[]{:S(2)}, u32[]{:S(2)}) %collective-permute-start.12) | collective-permute-done | bytes 262176 | tf_op jit(solution)/shard_map/ppermute | solution.py:14
  154.2 8.1 %collective-permute-done.13 = bf16[256,512]{0,1:T(8,128)(2,1)S(1)} collective-permute-done((bf16[256,512]{0,1:T(8,128)(2,1)S(1)}, bf16[256,512]{0,1:T(8,128)(2,1)S(1)}, u32[]{:S(2)}, u32[]{:S(2)}) %collective-permute-start.13) | collective-permute-done | bytes 262176 | tf_op jit(solution)/shard_map/ppermute | solution.py:14
  164.4 6.3 %collective-permute-done.14 = bf16[256,512]{0,1:T(8,128)(2,1)S(1)} collective-permute-done((bf16[256,512]{0,1:T(8,128)(2,1)S(1)}, bf16[256,512]{0,1:T(8,128)(2,1)S(1)}, u32[]{:S(2)}, u32[]{:S(2)}) %collective-permute-start.14) | collective-permute-done | bytes 262176 | tf_op jit(solution)/shard_map/ppermute | solution.py:14
  171.5 6.4 %copy.42 = bf16[256,64,128]{2,0,1:T(8,128)(2,1)} copy(bf16[256,64,128]{0,2,1:T(8,128)(2,1)} %bitcast) | data formatting | bytes 8388608 | tf_op jit(solution)/shard_map/reshape | solution.py:29
  177.8 8.5 %gather_fusion = bf16[112,256,128]{2,1,0:T(8,128)(2,1)} fusion(bf16[256,64,128]{2,0,1:T(8,128)(2,1)} %copy.42, s32[1024]{0:T(1024)S(1)} %pad_clamp_fusion.1), kind=kCustom, calls=%fused_computation | custom fusion | bytes 14680512 | tf_op jit(solution)/shard_map/gather | solution.py:31
  186.3 11.2 %copy.43 = bf16[7,16,256,128]{2,3,1,0:T(8,128)(2,1)} copy(bf16[7,16,256,128]{3,2,1,0:T(8,128)(2,1)} %bitcast.69) | data formatting | bytes 14680064 | tf_op jit(solution)/shard_map/gather | solution.py:31
  197.5 6.4 %copy.46 = bf16[256,64,128]{2,0,1:T(8,128)(2,1)} copy(bf16[256,64,128]{0,2,1:T(8,128)(2,1)} %bitcast.74) | data formatting | bytes 8388608 | tf_op jit(solution)/shard_map/reshape | solution.py:28
  203.9 8.7 %gather_fusion.1 = bf16[112,256,128]{2,1,0:T(8,128)(2,1)} fusion(bf16[256,64,128]{2,0,1:T(8,128)(2,1)} %copy.46, s32[1024]{0:T(1024)S(1)} %pad_clamp_fusion), kind=kCustom, calls=%fused_computation.1 | custom fusion | bytes 14680512 | tf_op jit(solution)/shard_map/gather | solution.py:30
  212.6 6.8 %convolution_bitcast_fusion = f32[256,7,128]{0,2,1:T(8,128)S(1)} fusion(bf16[7,16,128,128]{3,2,1,0:T(8,128)(2,1)} %param.8, bf16[256,7,16,128]{3,0,2,1:T(8,128)(2,1)} %bitcast.67), kind=kOutput, calls=%fused_computation.14 | convolution fusion | flops 939524096 | bytes 11927552 | tf_op jit(solution)/shard_map/tjkc,jkhc->tjh/dot_general | solution.py:32
  220.3 3.9 convert_bitcast_fusion
  224.2 6.6 %copy.53 = bf16[7,16,128,128]{3,1,0,2:T(8,128)(2,1)} copy(bf16[7,16,128,128]{2,3,1,0:T(8,128)(2,1)} %convert_bitcast_fusion) | data formatting | bytes 7340032 | tf_op jit(solution)/shard_map/convert_element_type | solution.py:48
  231.1 11.4 %copy.47 = bf16[7,16,256,128]{2,3,1,0:T(8,128)(2,1)} copy(bf16[7,16,256,128]{3,2,1,0:T(8,128)(2,1)} %bitcast.68) | data formatting | bytes 14680064 | tf_op jit(solution)/shard_map/gather | solution.py:30
  242.5 6.8 %fusion.17 = bf16[256,7,128]{0,2,1:T(8,128)(2,1)S(1)} fusion(bf16[7,16,128,128]{3,2,1,0:T(8,128)(2,1)} %param.10, bf16[256,7,16,128]{3,0,2,1:T(8,128)(2,1)} %bitcast.70, f32[256,7,128]{0,2,1:T(8,128)S(1)} %copy-done.2), kind=kOutput, calls=%fused_computation.18 | convolution fusion | flops 941588480 | bytes 12386304 | tf_op jit(solution)/shard_map/tjkc,jkhc->tjh/dot_general | solution.py:35
  249.4 3.9 convert_bitcast_fusion.1
  253.3 6.5 %copy.51 = bf16[7,16,128,128]{3,1,0,2:T(8,128)(2,1)} copy(bf16[7,16,128,128]{2,3,1,0:T(8,128)(2,1)} %convert_bitcast_fusion.1) | data formatting | bytes 7340032 | tf_op jit(solution)/shard_map/convert_element_type | solution.py:45
  259.9 11.3 %convolution_convert_fusion = bf16[7,64,128,128]{3,1,2,0:T(8,128)(2,1)} fusion(bf16[7,16,128,128]{3,2,1,0:T(8,128)(2,1)} %param.8, s32[7,16]{1,0:T(8,128)S(1)} %copy-done.3), kind=kOutput, calls=%fused_computation.6 | convolution fusion | flops 242228224 | bytes 18350528 | tf_op jit(solution)/shard_map/jkb,jkhc->jhbc/dot_general | solution.py:54
  271.2 17.6 %fusion.3 = bf16[256,8192]{1,0:T(8,128)(2,1)} fusion(bf16[256,896]{0,1:T(8,128)(2,1)S(1)} %bitcast.75, bf16[112,8,64,128]{3,2,1,0:T(8,128)(2,1)} %bitcast.71), kind=kOutput, calls=%fused_computation.5 | convolution fusion | flops 3760193536 | bytes 19333120 | tf_op jit(solution)/shard_map/dot_general | solution.py:59
  288.8 3.9 copy.55
  292.7 36.9 %reduce-scatter.6.cloned.1.call-done = bf16[7,16,64,128]{3,1,0,2:T(8,128)(2,1)} async-done(((bf16[7,16,128,128]{3,1,0,2:T(8,128)(2,1)}), bf16[7,16,64,128]{3,1,0,2:T(8,128)(2,1)}) %reduce-scatter.6.cloned.1.call-update) | async-done | bytes 1835024 | tf_op jit(solution)/shard_map/reduce_scatter | solution.py:44
  333.5 73.2 %reduce-scatter.4.cloned.1.call-done = bf16[256,512]{1,0:T(8,128)(2,1)} async-done(((bf16[256,8192]{1,0:T(8,128)(2,1)}), bf16[256,512]{1,0:T(8,128)(2,1)}) %reduce-scatter.4.cloned.1.call-update) | async-done | bytes 262160 | tf_op jit(solution)/shard_map/reduce_scatter | solution.py:60
  (63 shorter events, 25.9 us)
Async XLA Ops:
  7.2 190.3 %all-gather.2.cloned.1.call-start = ((), (), s32[]{:S(2)}) async-start(), calls=%async_computation.3 | async-start | bytes 4456448 | tf_op jit(solution)/shard_map/all_gather | solution.py:21
  9.0 279.8 %reduce-scatter.8.cloned.1.call-start = ((), (), s32[]{:S(2)}) async-start(), calls=%async_computation.6 | async-start | bytes 5505024 | tf_op jit(solution)/shard_map/reduce_scatter | solution.py:47
  10.2 11.5 %collective-permute-start = (bf16[256,512]{0,1:T(8,128)(2,1)S(1)}, bf16[256,512]{0,1:T(8,128)(2,1)S(1)}, u32[]{:S(2)}, u32[]{:S(2)}) collective-permute-start(bf16[256,512]{0,1:T(8,128)(2,1)S(1)} %copy.40), channel_id=1, source_target_pairs={{0,1},{1,2},{2,3},{3,4},{4,5},{5,6},{6,7},{7,8},{8,9},{9,10},{10,1... | collective-permute-start | bytes 786440 | tf_op jit(solution)/shard_map/ppermute | solution.py:14
  21.7 16.8 %collective-permute-start.1 = (bf16[256,512]{0,1:T(8,128)(2,1)S(1)}, bf16[256,512]{0,1:T(8,128)(2,1)S(1)}, u32[]{:S(2)}, u32[]{:S(2)}) collective-permute-start(bf16[256,512]{0,1:T(8,128)(2,1)S(1)} %collective-permute-done), channel_id=1, source_target_pairs={{0,1},{1,2},{2,3},{3,4},{4,5},{5,6},{6,7},{7,8},{8,9},{9,10},{10,1... | collective-permute-start | bytes 786440 | tf_op jit(solution)/shard_map/ppermute | solution.py:14
  38.5 10.9 %collective-permute-start.2 = (bf16[256,512]{0,1:T(8,128)(2,1)S(1)}, bf16[256,512]{0,1:T(8,128)(2,1)S(1)}, u32[]{:S(2)}, u32[]{:S(2)}) collective-permute-start(bf16[256,512]{0,1:T(8,128)(2,1)S(1)} %collective-permute-done.1), channel_id=1, source_target_pairs={{0,1},{1,2},{2,3},{3,4},{4,5},{5,6},{6,7},{7,8},{8,9},{9,10},{10,1... | collective-permute-start | bytes 786440 | tf_op jit(solution)/shard_map/ppermute | solution.py:14
  49.4 16.5 %collective-permute-start.3 = (bf16[256,512]{0,1:T(8,128)(2,1)S(1)}, bf16[256,512]{0,1:T(8,128)(2,1)S(1)}, u32[]{:S(2)}, u32[]{:S(2)}) collective-permute-start(bf16[256,512]{0,1:T(8,128)(2,1)S(1)} %collective-permute-done.2), channel_id=1, source_target_pairs={{0,1},{1,2},{2,3},{3,4},{4,5},{5,6},{6,7},{7,8},{8,9},{9,10},{10,1... | collective-permute-start | bytes 786440 | tf_op jit(solution)/shard_map/ppermute | solution.py:14
  65.9 11.7 %collective-permute-start.4 = (bf16[256,512]{0,1:T(8,128)(2,1)S(1)}, bf16[256,512]{0,1:T(8,128)(2,1)S(1)}, u32[]{:S(2)}, u32[]{:S(2)}) collective-permute-start(bf16[256,512]{0,1:T(8,128)(2,1)S(1)} %collective-permute-done.3), channel_id=1, source_target_pairs={{0,1},{1,2},{2,3},{3,4},{4,5},{5,6},{6,7},{7,8},{8,9},{9,10},{10,1... | collective-permute-start | bytes 786440 | tf_op jit(solution)/shard_map/ppermute | solution.py:14
  77.6 10.8 %collective-permute-start.5 = (bf16[256,512]{0,1:T(8,128)(2,1)S(1)}, bf16[256,512]{0,1:T(8,128)(2,1)S(1)}, u32[]{:S(2)}, u32[]{:S(2)}) collective-permute-start(bf16[256,512]{0,1:T(8,128)(2,1)S(1)} %collective-permute-done.4), channel_id=1, source_target_pairs={{0,1},{1,2},{2,3},{3,4},{4,5},{5,6},{6,7},{7,8},{8,9},{9,10},{10,1... | collective-permute-start | bytes 786440 | tf_op jit(solution)/shard_map/ppermute | solution.py:14
  88.4 10.2 %collective-permute-start.6 = (bf16[256,512]{0,1:T(8,128)(2,1)S(1)}, bf16[256,512]{0,1:T(8,128)(2,1)S(1)}, u32[]{:S(2)}, u32[]{:S(2)}) collective-permute-start(bf16[256,512]{0,1:T(8,128)(2,1)S(1)} %collective-permute-done.5), channel_id=1, source_target_pairs={{0,1},{1,2},{2,3},{3,4},{4,5},{5,6},{6,7},{7,8},{8,9},{9,10},{10,1... | collective-permute-start | bytes 786440 | tf_op jit(solution)/shard_map/ppermute | solution.py:14
  98.6 9.6 %collective-permute-start.7 = (bf16[256,512]{0,1:T(8,128)(2,1)S(1)}, bf16[256,512]{0,1:T(8,128)(2,1)S(1)}, u32[]{:S(2)}, u32[]{:S(2)}) collective-permute-start(bf16[256,512]{0,1:T(8,128)(2,1)S(1)} %collective-permute-done.6), channel_id=1, source_target_pairs={{0,1},{1,2},{2,3},{3,4},{4,5},{5,6},{6,7},{7,8},{8,9},{9,10},{10,1... | collective-permute-start | bytes 786440 | tf_op jit(solution)/shard_map/ppermute | solution.py:14
  108.2 9.0 %collective-permute-start.8 = (bf16[256,512]{0,1:T(8,128)(2,1)S(1)}, bf16[256,512]{0,1:T(8,128)(2,1)S(1)}, u32[]{:S(2)}, u32[]{:S(2)}) collective-permute-start(bf16[256,512]{0,1:T(8,128)(2,1)S(1)} %collective-permute-done.7), channel_id=1, source_target_pairs={{0,1},{1,2},{2,3},{3,4},{4,5},{5,6},{6,7},{7,8},{8,9},{9,10},{10,1... | collective-permute-start | bytes 786440 | tf_op jit(solution)/shard_map/ppermute | solution.py:14
  117.2 8.5 %collective-permute-start.9 = (bf16[256,512]{0,1:T(8,128)(2,1)S(1)}, bf16[256,512]{0,1:T(8,128)(2,1)S(1)}, u32[]{:S(2)}, u32[]{:S(2)}) collective-permute-start(bf16[256,512]{0,1:T(8,128)(2,1)S(1)} %collective-permute-done.8), channel_id=1, source_target_pairs={{0,1},{1,2},{2,3},{3,4},{4,5},{5,6},{6,7},{7,8},{8,9},{9,10},{10,1... | collective-permute-start | bytes 786440 | tf_op jit(solution)/shard_map/ppermute | solution.py:14
  125.7 8.5 %collective-permute-start.10 = (bf16[256,512]{0,1:T(8,128)(2,1)S(1)}, bf16[256,512]{0,1:T(8,128)(2,1)S(1)}, u32[]{:S(2)}, u32[]{:S(2)}) collective-permute-start(bf16[256,512]{0,1:T(8,128)(2,1)S(1)} %collective-permute-done.9), channel_id=1, source_target_pairs={{0,1},{1,2},{2,3},{3,4},{4,5},{5,6},{6,7},{7,8},{8,9},{9,10},{10,1... | collective-permute-start | bytes 786440 | tf_op jit(solution)/shard_map/ppermute | solution.py:14
  134.2 8.5 %collective-permute-start.11 = (bf16[256,512]{0,1:T(8,128)(2,1)S(1)}, bf16[256,512]{0,1:T(8,128)(2,1)S(1)}, u32[]{:S(2)}, u32[]{:S(2)}) collective-permute-start(bf16[256,512]{0,1:T(8,128)(2,1)S(1)} %collective-permute-done.10), channel_id=1, source_target_pairs={{0,1},{1,2},{2,3},{3,4},{4,5},{5,6},{6,7},{7,8},{8,9},{9,10},{10,1... | collective-permute-start | bytes 786440 | tf_op jit(solution)/shard_map/ppermute | solution.py:14
  142.7 9.3 %collective-permute-start.12 = (bf16[256,512]{0,1:T(8,128)(2,1)S(1)}, bf16[256,512]{0,1:T(8,128)(2,1)S(1)}, u32[]{:S(2)}, u32[]{:S(2)}) collective-permute-start(bf16[256,512]{0,1:T(8,128)(2,1)S(1)} %collective-permute-done.11), channel_id=1, source_target_pairs={{0,1},{1,2},{2,3},{3,4},{4,5},{5,6},{6,7},{7,8},{8,9},{9,10},{10,1... | collective-permute-start | bytes 786440 | tf_op jit(solution)/shard_map/ppermute | solution.py:14
  152.0 10.2 %collective-permute-start.13 = (bf16[256,512]{0,1:T(8,128)(2,1)S(1)}, bf16[256,512]{0,1:T(8,128)(2,1)S(1)}, u32[]{:S(2)}, u32[]{:S(2)}) collective-permute-start(bf16[256,512]{0,1:T(8,128)(2,1)S(1)} %collective-permute-done.12), channel_id=1, source_target_pairs={{0,1},{1,2},{2,3},{3,4},{4,5},{5,6},{6,7},{7,8},{8,9},{9,10},{10,1... | collective-permute-start | bytes 786440 | tf_op jit(solution)/shard_map/ppermute | solution.py:14
  162.2 8.5 %collective-permute-start.14 = (bf16[256,512]{0,1:T(8,128)(2,1)S(1)}, bf16[256,512]{0,1:T(8,128)(2,1)S(1)}, u32[]{:S(2)}, u32[]{:S(2)}) collective-permute-start(bf16[256,512]{0,1:T(8,128)(2,1)S(1)} %collective-permute-done.13), channel_id=1, source_target_pairs={{0,1},{1,2},{2,3},{3,4},{4,5},{5,6},{6,7},{7,8},{8,9},{9,10},{10,1... | collective-permute-start | bytes 786440 | tf_op jit(solution)/shard_map/ppermute | solution.py:14
  203.9 16.4 %slice-start = ((s8[7340032]{0:T(1024)(128)(4,1)}), s8[3145728]{0:T(1024)(128)(4,1)S(1)}, s32[]{:S(2)}) async-start(s8[7340032]{0:T(1024)(128)(4,1)} %bitcast.72), calls=%async_computation.7 | async-start | bytes 6291456
  212.6 7.7 %slice-start.1 = ((s8[7340032]{0:T(1024)(128)(4,1)}), s8[4194304]{0:T(1024)(128)(4,1)S(1)}, s32[]{:S(2)}) async-start(s8[7340032]{0:T(1024)(128)(4,1)} %bitcast.72), calls=%async_computation.8 | async-start | bytes 8388608
  219.3 0.9 copy-start.1
  230.9 98.7 %reduce-scatter.6.cloned.1.call-start = ((), (), s32[]{:S(2)}) async-start(), calls=%async_computation.5 | async-start | bytes 5505024 | tf_op jit(solution)/shard_map/reduce_scatter | solution.py:44
  231.1 11.4 %copy-start.2 = (f32[256,7,128]{0,2,1:T(8,128)S(1)}, f32[256,7,128]{0,2,1:T(8,128)}, u32[]{:S(2)}) copy-start(f32[256,7,128]{0,2,1:T(8,128)} %copy-done.1) | copy-start | bytes 2752516
  242.5 6.9 %copy-start = (bf16[7,16,256,128]{2,3,1,0:T(8,128)(2,1)S(1)}, bf16[7,16,256,128]{2,3,1,0:T(8,128)(2,1)}, u32[]{:S(2)}) copy-start(bf16[7,16,256,128]{2,3,1,0:T(8,128)(2,1)} %copy.47) | copy-start | bytes 22020100
  253.3 6.6 %copy-start.3 = (s32[7,16]{1,0:T(8,128)S(1)}, s32[7,16]{1,0:T(8,128)}, u32[]{:S(2)}) copy-start(s32[7,16]{1,0:T(8,128)} %param.9) | copy-start | bytes 1348
  259.8 146.8 %reduce-scatter.4.cloned.1.call-start = ((), (), s32[]{:S(2)}) async-start(), calls=%async_computation.4 | async-start | bytes 4456448 | tf_op jit(solution)/shard_map/reduce_scatter | solution.py:60
Sparse Core Ops, SparseCore 0:
  10.8 61.8 all-gather.1
  231.0 46.5 reduce-scatter.7
  280.4 49.1 reduce-scatter.5
  333.9 72.7 reduce-scatter.3
